TPU v7x, 128 devices: a whole 4x4x4 slice. The times are simulated.
128 devices in a mesh: clus: 8 (over x, core), trow: 4 (over y), tcol: 4 (over z).
Axes of the slice: x: 4, y: 4, z: 4, core: 2. Of those that a mesh axis runs over, the one named last changes fastest.
Arguments:
- embeddings: bfloat16 [65536, 1024], P(('clus', 'trow', 'tcol'))
- target: int32 [65536], P(('clus', 'trow', 'tcol')), may hold values from 0 to 98303, as said below
Outputs:
- best_cosine: float32 [65536], P(('clus', 'trow', 'tcol'))
Inputs may be any that keep to these rules, and one draw needn't show every extreme that they name: `target`: the grid has 8 clusters of 12288 slots each; the rows of a cluster fill its slots 0 to its size - 1, each slot once; every cluster has a row, and the last cluster is the largest and fills all 12288 slots. The rows of one device send at most 6 rows to any aligned block of 768 slots, and some block receives exactly 6 from every device.
All inputs are finite; a program needn't handle non-finite values.
Results may differ from a plain program's by a relative error of at most 0.00069.
Values may be sent and summed in bfloat16 or wider, within the bound.
A program may use at most 128 MiB of HBM per device.

v0:
```python
import jax
import jax.numpy as jnp
from jax import lax
from jax.sharding import PartitionSpec as P

SLOTS = 768
epsilon = 1e-06
ABSENT = 4.0


def on_device(embeddings, target):
    width = embeddings.shape[1]
    clusters_count = lax.axis_size("clus")
    tile_rows = lax.axis_size("trow")
    tile_cols = lax.axis_size("tcol")
    group_count = tile_rows * tile_cols
    devices = clusters_count * group_count
    pair_rows = SLOTS // devices
    values = embeddings.astype(jnp.float32)
    unit_rows = (
        values / jnp.sqrt(jnp.sum(values * values, axis=1, keepdims=True) + epsilon)
    ).astype(jnp.bfloat16)
    destination = target // SLOTS
    onehot = (destination[:, None] == jnp.arange(devices, dtype=jnp.int32)[None, :]).astype(
        jnp.int32
    )
    position = jnp.sum(onehot * (jnp.cumsum(onehot, axis=0) - 1), axis=1)
    buffer_slot = destination * pair_rows + position
    outgoing = jnp.full((SLOTS, width), ABSENT, jnp.bfloat16).at[buffer_slot].set(unit_rows)
    arrived = lax.all_to_all(
        outgoing.reshape(devices, pair_rows, width),
        ("clus", "trow", "tcol"),
        split_axis=0,
        concat_axis=0,
        tiled=True,
    ).reshape(SLOTS, width)
    row_pos = lax.axis_index("trow")
    col_pos = lax.axis_index("tcol")
    row_block = lax.all_gather(arrived, "tcol", axis=0, tiled=True)
    col_block = lax.all_gather(arrived, "trow", axis=0, tiled=True)
    local = jnp.arange(SLOTS, dtype=jnp.int32)
    row_index = (
        (row_pos * tile_cols + jnp.arange(tile_cols, dtype=jnp.int32))[:, None] * SLOTS
        + local[None, :]
    ).reshape(-1)
    col_index = (
        (jnp.arange(tile_rows, dtype=jnp.int32) * tile_cols + col_pos)[:, None] * SLOTS
        + local[None, :]
    ).reshape(-1)
    present = col_block[:, 0].astype(jnp.float32) < 2.0
    scores = lax.dot_general(
        row_block, col_block, (((1,), (1,)), ((), ())), preferred_element_type=jnp.float32
    )
    keep = present[None, :] & (col_index[None, :] != row_index[:, None])
    partial = jnp.max(jnp.where(keep, scores, -1.0), axis=1)
    outbound = partial.reshape(tile_cols, devices, pair_rows).transpose(1, 0, 2)
    returned = lax.all_to_all(
        outbound, ("clus", "trow", "tcol"), split_axis=0, concat_axis=0, tiled=True
    )
    best = jnp.max(
        returned.reshape(clusters_count, tile_rows, tile_cols, tile_cols, pair_rows), axis=2
    ).reshape(SLOTS)
    return best[buffer_slot]


def solution(mesh):
    in_specs = (P(("clus", "trow", "tcol"), None), P(("clus", "trow", "tcol")))
    out_specs = P(("clus", "trow", "tcol"))
    return jax.shard_map(
        on_device, mesh=mesh, in_specs=in_specs, out_specs=out_specs, check_vma=False
    )
```

profile of v0, /device:TPU:1, one launch (start us, length us, event | category | flops | bytes accessed | tf_op | source)
XLA Modules:
  0.0 249.8 jit_solution(1314348164494295271)
XLA Ops:
  6.5 0.7 fusion.14
  7.2 0.7 add_select_fusion
  7.9 0.1 copy.5
  8.0 0.2 fusion.8
  8.4 0.2 fusion.7
  8.6 0.7 compare_select_fusion
  9.3 1.5 fusion
  10.8 4.6 %scatter_custom_fusion = bf16[768,1024]{1,0:T(8,128)(2,1)} fusion(s32[512]{0:T(512)S(1)} %compare_select_fusion, bf16[512,1024]{1,0:T(8,128)(2,1)} %param.2, f32[512]{0:T(512)S(1)} %add_sqrt_fusion, bf16[]{:T(256)} %constant.14.clone.1), kind=kCustom, calls=%fused_computation.9 | custom fusion | flops 1572864 | bytes 2623490 | tf_op jit(solution)/shard_map/scatter | solution.py:29
  15.4 2.5 reshape.90
  17.9 40.8 %all_to_all.10 = bf16[128,6,1024]{2,1,0:T(8,128)(2,1)} all-to-all(bf16[128,6,1024]{2,1,0:T(8,128)(2,1)S(1)} %reshape.90), channel_id=1, replica_groups=mesh['clus'=8,'trow'=4,'tcol'=4] {'clus','trow','tcol'}, dimensions={0} | all-to-all | bytes 3145728 | tf_op jit(solution)/shard_map/all_to_all | solution.py:30
  58.7 3.7 %reshape.91 = bf16[768,1024]{1,0:T(8,128)(2,1)} reshape(bf16[128,6,1024]{2,1,0:T(8,128)(2,1)} %all_to_all.10) | data formatting | bytes 3145728 | tf_op jit(solution)/shard_map/reshape | solution.py:36
  62.4 0.7 all-gather.5.cloned.1.call-update
  63.2 0.1 iota_add_fusion
  63.2 0.1 iota_add_fusion.1
  63.3 61.4 %all-gather.3.cloned.1.call-done = bf16[3072,1024]{1,0:T(8,128)(2,1)} async-done(((bf16[768,1024]{1,0:T(8,128)(2,1)}), bf16[3072,1024]{1,0:T(8,128)(2,1)}) %all-gather.3.cloned.1.call-update) | async-done | bytes 6291472 | tf_op jit(solution)/shard_map/all_gather | solution.py:40
  124.8 1.6 fusion.2
  126.4 66.6 %all-gather.5.cloned.1.call-done = bf16[3072,1024]{1,0:T(8,128)(2,1)} async-done(((bf16[768,1024]{1,0:T(8,128)(2,1)}), bf16[3072,1024]{1,0:T(8,128)(2,1)}) %all-gather.5.cloned.1.call-update) | async-done | bytes 6291472 | tf_op jit(solution)/shard_map/all_gather | solution.py:39
  193.0 25.1 %select_reduce_fusion = f32[3072]{0:T(1024)S(1)} fusion(bf16[3072,1024]{1,0:T(8,128)(2,1)} %all-gather.5.cloned.1.call-done, bf16[3072,1024]{1,0:T(8,128)(2,1)} %all-gather.3.cloned.1.call-done, s32[3072]{0:T(1024)S(1)} %add.97, s32[3072]{0:T(1024)S(1)} %add.91, pred[3072]{0:T(1024)(128)(4,1)S(1)} %fusion.2), kind=kOutput, calls=%fused_computation.2 | convolution fusion | flops 19365097472 | bytes 12622848 | tf_op jit(solution)/shard_map/dot_general | solution.py:51
  218.1 0.2 reshape.92
  218.3 0.9 copy.7
  219.2 8.9 %all-to-all-start.1 = ((f32[128,4,6]{2,1,0:T(4,128)}), f32[128,4,6]{2,1,0:T(4,128)S(1)}, u32[]{:S(2)}, u32[]{:S(2)}) async-start(f32[128,4,6]{2,1,0:T(4,128)} %copy.7), calls=%async_computation.1 | async-start | bytes 524288 | tf_op jit(solution)/shard_map/all_to_all | solution.py:57
  228.1 11.2 %all-to-all-done.1 = f32[128,4,6]{2,1,0:T(4,128)S(1)} async-done(((f32[128,4,6]{2,1,0:T(4,128)}), f32[128,4,6]{2,1,0:T(4,128)S(1)}, u32[]{:S(2)}, u32[]{:S(2)}) %all-to-all-start.1) | async-done | bytes 12320 | tf_op jit(solution)/shard_map/all_to_all | solution.py:57
  239.4 0.1 reshape.94
  239.5 3.4 %gather_fusion = f32[512]{0:T(512)} fusion(f32[768]{0:T(1024)S(1)} %reshape.94, s32[1024]{0:T(1024)S(1)} %pad_clamp_fusion), kind=kCustom, calls=%fused_computation | custom fusion | bytes 6144 | tf_op jit(solution)/shard_map/gather | solution.py:63
  (15 shorter events, 0.3 us)
Async XLA Ops:
  6.5 118.2 %all-gather.3.cloned.1.call-start = ((), (), s32[]{:S(2)}) async-start(), calls=%async_computation.2 | async-start | bytes 7864320 | tf_op jit(solution)/shard_map/all_gather | solution.py:40
  62.4 130.6 %all-gather.5.cloned.1.call-start = ((), (), s32[]{:S(2)}) async-start(), calls=%async_computation.3 | async-start | bytes 7864320 | tf_op jit(solution)/shard_map/all_gather | solution.py:39
  219.2 20.2 %all-to-all-start.1 = ((f32[128,4,6]{2,1,0:T(4,128)}), f32[128,4,6]{2,1,0:T(4,128)S(1)}, u32[]{:S(2)}, u32[]{:S(2)}) async-start(f32[128,4,6]{2,1,0:T(4,128)} %copy.7), calls=%async_computation.1 | async-start | bytes 524288 | tf_op jit(solution)/shard_map/all_to_all | solution.py:57
Sparse Core Ops, SparseCore 0:
  62.5 62.2 all-gather.2
  126.4 66.4 all-gather.4
where the time goes:
time: 250 us
  waiting for transfers between devices  140 us (56%)
  blocking collectives  40.8 us (16%)
  matrix products  25.1 us (10%)
  between operations  13.5 us (5%)
  local copies, waits for them, and re-layouts  11 us (4%)
  other arithmetic  10.6 us (4%)
  starting transfers between devices  8.98 us (4%)
    all_gather x1, waiting for transfers between devices, on_device(): row_block = lax.all_gather(arrived, 'tcol', axis=0, tiled=True)  66.6 us
    all_gather x1, waiting for transfers between devices, on_device(): col_block = lax.all_gather(arrived, 'trow', axis=0, tiled=True)  61.4 us
    all_to_all x1, blocking collectives, on_device(): lax.all_to_all(outgoing.reshape(devices, pair_rows, width), ('clus', 'tro...  40.8 us
    dot_general x1, matrix products, on_device(): lax.dot_general(row_block, col_block, (((1,), (1,)), ((), ())), preferred...  25.1 us
    all_to_all x1, waiting for transfers between devices, on_device(): lax.all_to_all(outbound, ('clus', 'trow', 'tcol'), split_axis=0, concat_a...  11.2 us
    all_to_all x1, starting transfers between devices, on_device(): lax.all_to_all(outbound, ('clus', 'trow', 'tcol'), split_axis=0, concat_a...  8.94 us
  transfers between devices with their start and end apart: 3, of which 3 were waited for; matrix products, arithmetic and copies ran while one was open for 1% of the time, Pallas kernels for 0%

commit v1 on v0

--- a/solution.py
+++ b/solution.py
@@ -6,6 +6,27 @@
 SLOTS = 768
 epsilon = 1e-06
 ABSENT = 4.0
+
+
+def collect(x, axis, dim):
+    size, mine, width = (lax.axis_size(axis), lax.axis_index(axis), x.shape[dim])
+    upward = [(i, (i + 1) % size) for i in range(size)]
+    backward = [(i, (i - 1) % size) for i in range(size)]
+    out = jnp.zeros((*x.shape[:dim], size * width, *x.shape[dim + 1 :]), x.dtype)
+    out = lax.dynamic_update_slice_in_dim(out, x, mine * width, axis=dim)
+    from_left = from_right = x
+    middle = size // 2
+    for step in range(1, middle + 1):
+        from_left = lax.ppermute(from_left, axis, upward)
+        out = lax.dynamic_update_slice_in_dim(
+            out, from_left, (mine - step) % size * width, axis=dim
+        )
+        if step < size - middle:
+            from_right = lax.ppermute(from_right, axis, backward)
+            out = lax.dynamic_update_slice_in_dim(
+                out, from_right, (mine + step) % size * width, axis=dim
+            )
+    return out
 
 
 def on_device(embeddings, target):
@@ -36,7 +57,7 @@
     ).reshape(SLOTS, width)
     row_pos = lax.axis_index("trow")
     col_pos = lax.axis_index("tcol")
-    row_block = lax.all_gather(arrived, "tcol", axis=0, tiled=True)
+    row_block = collect(arrived, "tcol", 0)
     col_block = lax.all_gather(arrived, "trow", axis=0, tiled=True)
     local = jnp.arange(SLOTS, dtype=jnp.int32)
     row_index = (

time: 250 us -> 195 us (0.78)
  waiting for transfers between devices: 140 us -> 70.6 us
  local copies, waits for them, and re-layouts: 11 us -> 22.4 us
  starting transfers between devices: 8.98 us -> 11.6 us
    all_gather x1 -> x0, waiting for transfers between devices: 66.6 us -> none  [on_device(): row_block = lax.all_gather(arrived, 'tcol', axis=0, tiled=True)]
    all_gather x1, waiting for transfers between devices: 61.4 us -> 0.01 us  [on_device(): col_block = lax.all_gather(arrived, 'trow', axis=0, tiled=True)]
    ppermute x0 -> x3, waiting for transfers between devices: none -> 59.4 us  [the longest x2 59.3 us: collect(): from_left = lax.ppermute(from_left, axis, upward)]
    dynamic_update_slice x0 -> x4, local copies, waits for them, and re-layouts: none -> 8.01 us  [the longest x2 3.95 us: collect(): lax.dynamic_update_slice_in_dim(out, from_left, (mine - step) % size * wi...]
    broadcast_in_dim x0 -> x1, local copies, waits for them, and re-layouts: none -> 3.46 us  [collect(): out = jnp.zeros((*x.shape[:dim], size * width, *x.shape[dim + 1:]), x.dtype)]
    ppermute x0 -> x3, starting transfers between devices: none -> 2.75 us  [the longest x1 1.82 us: collect(): from_right = lax.ppermute(from_right, axis, backward)]
  transfers between devices with their start and end apart: 3 -> 5, of which waited for: 3 -> 3; matrix products, arithmetic and copies ran while one was open for 1% -> 6% of each run, Pallas kernels for 0% -> 0%
where the time goes in v1:
time: 195 us
  waiting for transfers between devices  70.6 us (36%)
  blocking collectives  40.8 us (21%)
  matrix products  25.1 us (13%)
  local copies, waits for them, and re-layouts  22.4 us (11%)
  between operations  13.5 us (7%)
  starting transfers between devices  11.6 us (6%)
  other arithmetic  10.6 us (5%)
    ppermute x2, waiting for transfers between devices, collect(): from_left = lax.ppermute(from_left, axis, upward)  59.3 us
    all_to_all x1, blocking collectives, on_device(): lax.all_to_all(outgoing.reshape(devices, pair_rows, width), ('clus', 'tro...  40.8 us
    dot_general x1, matrix products, on_device(): lax.dot_general(row_block, col_block, (((1,), (1,)), ((), ())), preferred...  25.1 us
    all_to_all x1, waiting for transfers between devices, on_device(): lax.all_to_all(outbound, ('clus', 'trow', 'tcol'), split_axis=0, concat_a...  11.2 us
    all_to_all x1, starting transfers between devices, on_device(): lax.all_to_all(outbound, ('clus', 'trow', 'tcol'), split_axis=0, concat_a...  8.84 us
    scatter x1, other arithmetic, on_device(): jnp.full((SLOTS, width), ABSENT, jnp.bfloat16).at[buffer_slot]  4.59 us
    dynamic_update_slice x2, local copies, waits for them, and re-layouts, collect(): lax.dynamic_update_slice_in_dim(out, from_left, (mine - step) % size * wi...  3.95 us
  transfers between devices with their start and end apart: 5, of which 3 were waited for; matrix products, arithmetic and copies ran while one was open for 6% of the time, Pallas kernels for 0%

profile of v1, /device:TPU:1, one launch (start us, length us, event | category | flops | bytes accessed | tf_op | source)
XLA Modules:
  0.0 194.5 jit_solution(5053925908349976161)
XLA Ops:
  6.5 0.7 fusion.14
  7.2 0.7 add_select_fusion
  8.4 0.2 fusion.7
  8.6 0.7 compare_select_fusion
  9.3 1.5 fusion
  10.8 4.6 %scatter_custom_fusion = bf16[768,1024]{1,0:T(8,128)(2,1)} fusion(s32[512]{0:T(512)S(1)} %compare_select_fusion, bf16[512,1024]{1,0:T(8,128)(2,1)} %param.2, f32[512]{0:T(512)S(1)} %add_sqrt_fusion, bf16[]{:T(256)} %constant.54.clone.1), kind=kCustom, calls=%fused_computation.9 | custom fusion | flops 1572864 | bytes 2623490 | tf_op jit(solution)/shard_map/scatter | solution.py:50
  15.4 2.5 %reshape.90 = bf16[128,6,1024]{2,1,0:T(8,128)(2,1)S(1)} reshape(bf16[768,1024]{1,0:T(8,128)(2,1)} %scatter_custom_fusion) | data formatting | bytes 3145728 | tf_op jit(solution)/shard_map/reshape | solution.py:52
  17.9 40.8 %all_to_all.10 = bf16[128,6,1024]{2,1,0:T(8,128)(2,1)} all-to-all(bf16[128,6,1024]{2,1,0:T(8,128)(2,1)S(1)} %reshape.90), channel_id=1, replica_groups=mesh['clus'=8,'trow'=4,'tcol'=4] {'clus','trow','tcol'}, dimensions={0} | all-to-all | bytes 3145728 | tf_op jit(solution)/shard_map/all_to_all | solution.py:51
  58.7 3.7 %reshape.91 = bf16[768,1024]{1,0:T(8,128)(2,1)} reshape(bf16[128,6,1024]{2,1,0:T(8,128)(2,1)} %all_to_all.10) | data formatting | bytes 3145728 | tf_op jit(solution)/shard_map/reshape | solution.py:57
  62.4 0.9 collective-permute-start
  63.3 1.8 collective-permute-start.1
  65.1 33.3 %collective-permute-done = bf16[768,1024]{1,0:T(8,128)(2,1)S(1)} collective-permute-done((bf16[768,1024]{1,0:T(8,128)(2,1)}, bf16[768,1024]{1,0:T(8,128)(2,1)S(1)}, u32[]{:S(2)}, u32[]{:S(2)}) %collective-permute-start) | collective-permute-done | bytes 1572896 | tf_op jit(solution)/shard_map/ppermute | solution.py:20
  98.7 3.5 %broadcast_in_dim.11 = bf16[3072,1024]{1,0:T(8,128)(2,1)} broadcast(bf16[]{:T(256)} %constant.66.clone.1), dimensions={} | broadcast | bytes 6291458 | tf_op jit(solution)/shard_map/broadcast_in_dim | solution.py:15
  102.1 1.3 constant_dynamic-update-slice_fusion.2
  103.4 1.3 constant_dynamic-update-slice_fusion.1
  104.6 2.8 %constant_dynamic-update-slice_fusion = bf16[3072,1024]{1,0:T(8,128)(2,1)} fusion(bf16[3072,1024]{1,0:T(8,128)(2,1)} %constant_dynamic-update-slice_fusion.1, bf16[768,1024]{1,0:T(8,128)(2,1)} %collective-permute-done.1, s32[]{:T(128)S(6)} %select_n.46), kind=kLoop, calls=%fused_computation.31 | loop fusion | bytes 3145732 | tf_op jit(solution)/shard_map/dynamic_update_slice | solution.py:26
  107.4 26.0 %collective-permute-done.2 = bf16[768,1024]{1,0:T(8,128)(2,1)} collective-permute-done((bf16[768,1024]{1,0:T(8,128)(2,1)S(1)}, bf16[768,1024]{1,0:T(8,128)(2,1)}, u32[]{:S(2)}, u32[]{:S(2)}) %collective-permute-start.2) | collective-permute-done | bytes 1572896 | tf_op jit(solution)/shard_map/ppermute | solution.py:20
  133.5 2.7 %constant_dynamic-update-slice_fusion.3 = bf16[3072,1024]{1,0:T(8,128)(2,1)} fusion(bf16[3072,1024]{1,0:T(8,128)(2,1)} %constant_dynamic-update-slice_fusion, bf16[768,1024]{1,0:T(8,128)(2,1)} %collective-permute-done.2, s32[]{:T(128)S(6)} %select_n.48), kind=kLoop, calls=%fused_computation.34 | loop fusion | bytes 3145732 | tf_op jit(solution)/shard_map/dynamic_update_slice | solution.py:21
  136.2 1.6 fusion.2
  137.8 25.1 %select_reduce_fusion = f32[3072]{0:T(1024)S(1)} fusion(bf16[3072,1024]{1,0:T(8,128)(2,1)} %constant_dynamic-update-slice_fusion.3, bf16[3072,1024]{1,0:T(8,128)(2,1)} %all-gather.2.cloned.1.call-done, s32[3072]{0:T(1024)S(1)} %add.124, s32[3072]{0:T(1024)S(1)} %add.118, pred[3072]{0:T(1024)(128)(4,1)S(1)} %fusion.2), kind=kOutput, calls=%fused_computation.2 | convolution fusion | flops 19365097472 | bytes 12622848 | tf_op jit(solution)/shard_map/dot_general | solution.py:72
  163.1 0.9 copy.7
  164.0 8.8 %all-to-all-start.1 = ((f32[128,4,6]{2,1,0:T(4,128)}), f32[128,4,6]{2,1,0:T(4,128)S(1)}, u32[]{:S(2)}, u32[]{:S(2)}) async-start(f32[128,4,6]{2,1,0:T(4,128)} %copy.7), calls=%async_computation.1 | async-start | bytes 524288 | tf_op jit(solution)/shard_map/all_to_all | solution.py:78
  172.8 11.2 %all-to-all-done.1 = f32[128,4,6]{2,1,0:T(4,128)S(1)} async-done(((f32[128,4,6]{2,1,0:T(4,128)}), f32[128,4,6]{2,1,0:T(4,128)S(1)}, u32[]{:S(2)}, u32[]{:S(2)}) %all-to-all-start.1) | async-done | bytes 12320 | tf_op jit(solution)/shard_map/all_to_all | solution.py:78
  184.3 3.4 %gather_fusion = f32[512]{0:T(512)} fusion(f32[768]{0:T(1024)S(1)} %reshape.94, s32[1024]{0:T(1024)S(1)} %pad_clamp_fusion), kind=kCustom, calls=%fused_computation | custom fusion | bytes 6144 | tf_op jit(solution)/shard_map/gather | solution.py:84
  (25 shorter events, 1.1 us)
Async XLA Ops:
  6.5 129.6 %all-gather.2.cloned.1.call-start = ((), (), s32[]{:S(2)}) async-start(), calls=%async_computation.2 | async-start | bytes 7864320 | tf_op jit(solution)/shard_map/all_gather | solution.py:61
  62.4 39.8 %copy-start = (bf16[768,1024]{1,0:T(8,128)(2,1)S(1)}, bf16[768,1024]{1,0:T(8,128)(2,1)}, u32[]{:S(2)}) copy-start(bf16[768,1024]{1,0:T(8,128)(2,1)} %reshape.91) | copy-start | bytes 4718596
  62.4 36.1 %collective-permute-start = (bf16[768,1024]{1,0:T(8,128)(2,1)}, bf16[768,1024]{1,0:T(8,128)(2,1)S(1)}, u32[]{:S(2)}, u32[]{:S(2)}) collective-permute-start(bf16[768,1024]{1,0:T(8,128)(2,1)} %reshape.91), channel_id=1, source_target_pairs={{0,1},{1,2},{2,3},{3,0},{4,5},{5,6},{6,7},{7,4},{8,9},{9,10},{10,1... | collective-permute-start | bytes 4718600 | tf_op jit(solution)/shard_map/ppermute | solution.py:20
  63.3 41.3 %collective-permute-start.1 = (bf16[768,1024]{1,0:T(8,128)(2,1)}, bf16[768,1024]{1,0:T(8,128)(2,1)}, u32[]{:S(2)}, u32[]{:S(2)}) collective-permute-start(bf16[768,1024]{1,0:T(8,128)(2,1)} %reshape.91), channel_id=1, source_target_pairs={{0,3},{1,0},{2,1},{3,2},{4,7},{5,4},{6,5},{7,6},{8,11},{9,8},{10,9... | collective-permute-start | bytes 4718600 | tf_op jit(solution)/shard_map/ppermute | solution.py:25
  98.4 35.0 %collective-permute-start.2 = (bf16[768,1024]{1,0:T(8,128)(2,1)S(1)}, bf16[768,1024]{1,0:T(8,128)(2,1)}, u32[]{:S(2)}, u32[]{:S(2)}) collective-permute-start(bf16[768,1024]{1,0:T(8,128)(2,1)S(1)} %collective-permute-done), channel_id=1, source_target_pairs={{0,1},{1,2},{2,3},{3,0},{4,5},{5,6},{6,7},{7,4},{8,9},{9,10},{10,1... | collective-permute-start | bytes 4718600 | tf_op jit(solution)/shard_map/ppermute | solution.py:20
  164.0 20.1 %all-to-all-start.1 = ((f32[128,4,6]{2,1,0:T(4,128)}), f32[128,4,6]{2,1,0:T(4,128)S(1)}, u32[]{:S(2)}, u32[]{:S(2)}) async-start(f32[128,4,6]{2,1,0:T(4,128)} %copy.7), calls=%async_computation.1 | async-start | bytes 524288 | tf_op jit(solution)/shard_map/all_to_all | solution.py:78
Sparse Core Ops, SparseCore 0:
  62.5 62.2 all-gather.1
